TPU v7x, 32 devices: a whole 2x2x4 slice. The times are simulated.
32 devices in a mesh: dp: 4 (over x, core), tm: 8 (over z, y).
Axes of the slice: x: 2, y: 2, z: 4, core: 2. Of those that a mesh axis runs over, the one named last changes fastest.
Arguments:
- latent: float32 [4, 64, 4096], P('dp', None, 'tm'), may hold values from -40 to 40
- target: float32 [4, 8192], P('dp', 'tm'), may hold values from -20 to 20
- up_kernel: float32 [4, 32, 64], replicated, may hold values from -0.5 to 0.5
- inner_kernel: float32 [3, 16, 32], replicated, may hold values from -0.625 to 0.625
- outer_kernel: float32 [32, 16], replicated, may hold values from -1.5 to 1.5
- out_kernel: float32 [7, 32], replicated, may hold values from -0.375 to 0.375
Outputs:
- latent_grad: float32 [4, 64, 4096], P('dp', None, 'tm')
- up_update: float32 [4, 32, 64], replicated
- inner_update: float32 [3, 16, 32], replicated
- outer_update: float32 [32, 16], replicated
- out_update: float32 [7, 32], replicated
All inputs are finite; a program needn't handle non-finite values.
Results may differ from a plain program's by a relative error of at most 0.0003.
Values sent between devices are 32-bit elements; how exact they have to be, the bound alone decides.
No kernel may reach another device: no remote copies, remote signals or barrier semaphores. Data moves between devices by JAX's collectives and lax.ppermute only.
A program may use at most 64 MiB of HBM per device.

v0:
```python
import jax
import jax.numpy as jnp
from jax import lax
from jax.sharding import PartitionSpec as P

MELS = 64
WIN_COARSE = 1024
WIN_FINE = 256
LOSS_WEIGHTS = (0.25, 0.5, 0.5)


def padded_2(cells, sides, width):
    for axis, dim in sides:
        count = lax.axis_size(axis)
        ends = count - 1
        head = lax.slice_in_dim(cells, 0, width, axis=dim)
        tail = lax.slice_in_dim(cells, cells.shape[dim] - width, cells.shape[dim], axis=dim)
        cells = jnp.concatenate(
            [
                lax.ppermute(tail, axis, [(i, (i + 1) % count) for i in range(ends)]),
                cells,
                lax.ppermute(head, axis, [((i + 1) % count, i) for i in range(ends)]),
            ],
            axis=dim,
        )
    return cells


def from_behind(x, axis, by):
    peers = lax.axis_size(axis)
    pairs = [(i, i + by) for i in range(peers) if 0 <= i + by < peers]
    return lax.ppermute(x, axis, pairs)


def product(form, left, right):
    return jnp.einsum(
        form, left, right, precision=lax.Precision.HIGHEST, preferred_element_type=jnp.float32
    )


def mel_bank(window, mel_count):
    half_window = window // 2
    top_mel = 2595.0 * jnp.log10(1.0 + 12000.0 / 700.0)
    points = (jnp.arange(mel_count + 1, dtype=jnp.float32) + 1.0) / (mel_count + 2.0) * top_mel
    centers = 700.0 * (jnp.power(10.0, points / 2595.0) - 1.0) / 12000.0 * half_window
    spacing = jnp.maximum(centers[1:] - centers[:-1], 1.0)
    places = jnp.arange(half_window, dtype=jnp.float32)[:, None]
    return jnp.maximum(0.0, 1.0 - jnp.abs(places - centers[None, :mel_count]) / spacing[None, :])


def dft_table(window):
    half_window = window // 2
    sample = jnp.arange(window, dtype=jnp.int32)[:, None]
    freq_index = jnp.arange(half_window, dtype=jnp.int32)[None, :]
    angles = (sample * freq_index % window).astype(jnp.float32) * (2.0 * jnp.pi / window)
    hann_taper = 0.5 - 0.5 * jnp.cos(sample.astype(jnp.float32) * (2.0 * jnp.pi / window))
    return jnp.concatenate([hann_taper * jnp.cos(angles), -hann_taper * jnp.sin(angles)], axis=1)


def framed(signal, window, frame_count):
    hop_size = window // 4
    blocks = signal.reshape(signal.shape[:-1] + (frame_count + 3, hop_size))
    return jnp.concatenate(
        [blocks[..., offset : offset + frame_count, :] for offset in range(4)], axis=-1
    )


def mel_energy(signal, window, frame_count):
    frames = framed(signal, window, frame_count)
    spectra = product("...nf,fk->...nk", frames, dft_table(window))
    half_window = window // 2
    energy = spectra[..., :half_window] ** 2 + spectra[..., half_window:] ** 2
    return product("...nk,km->...nm", energy, mel_bank(window, MELS))


def spectral_loss(signal, target_mel, window, frame_count):
    level = jnp.sqrt(mel_energy(signal, window, frame_count) + 1.0)
    return jnp.sum((level - jnp.sqrt(target_mel + 1.0)) ** 2)


def elu_slope(values):
    return jnp.where(values > 0, 1.0, jnp.exp(jnp.minimum(values, 0.0)))


def apply_mask(values, mask):
    return values * mask


def upsample_forward(values, kernel, stride, previous):
    lagged = jnp.concatenate([previous, values[:, :, :-1]], axis=2)
    phases = product("pij,bjm->bimp", kernel[:stride], values) + product(
        "pij,bjm->bimp", kernel[stride:], lagged
    )
    return (phases.reshape(phases.shape[0], phases.shape[1], -1), lagged)


def taps_forward(padded, kernel, length):
    summed = product("oi,bil->bol", kernel[0], padded[:, :, :length])
    for offset in range(1, kernel.shape[0]):
        summed = summed + product(
            "oi,bil->bol", kernel[offset], padded[:, :, offset : offset + length]
        )
    return summed


def decode_forward(activated, weights, movers, clip_mask):
    up_kernel, inner_kernel, outer_kernel, out_kernel = weights
    lend_frame, border_inner, border_output = movers
    upper, lagged = upsample_forward(activated, up_kernel, 2, lend_frame(activated[:, :, -1:]))
    upper = apply_mask(upper, clip_mask)
    padded_inner = border_inner(jax.nn.elu(upper))
    inner_out = taps_forward(padded_inner, inner_kernel, upper.shape[2])
    hidden = jax.nn.elu(inner_out)
    mixed = apply_mask(upper + product("oi,bil->bol", outer_kernel, hidden), clip_mask)
    padded_output = border_output(jax.nn.elu(mixed))
    waveform = taps_forward(padded_output, out_kernel[:, None, :], upper.shape[2])[:, 0, :]
    return (waveform, (upper, lagged, padded_inner, inner_out, hidden, mixed, padded_output))


def taps_backward(grad_out, padded, kernel, length, keep):
    tap_count = kernel.shape[0]
    row_grad = apply_mask(grad_out, keep)
    kernel_rows = jnp.stack(
        [
            product("nbol,bil->nboi", row_grad, padded[:, :, offset : offset + length])
            for offset in range(tap_count)
        ],
        axis=2,
    )
    spread = jnp.zeros(grad_out.shape[:2] + (kernel.shape[2], length + tap_count - 1), jnp.float32)
    for offset in range(tap_count):
        moved = product("oi,nbol->nbil", kernel[offset], grad_out)
        spread = spread + jnp.pad(moved, ((0, 0), (0, 0), (0, 0), (offset, tap_count - 1 - offset)))
    return (kernel_rows, spread)


def rims_backward(spread, rim_width):
    interior = spread[..., rim_width:-rim_width]
    return interior


def residual_backward(
    grad_mixed, upper, padded, inner_out, hidden, inner_kernel, outer_kernel, keep
):
    length = upper.shape[-1]
    outer_rows = product("nbol,bil->nboi", apply_mask(grad_mixed, keep), hidden)
    grad_inner = product("oi,nbol->nbil", outer_kernel, grad_mixed) * elu_slope(inner_out)
    inner_rows, spread = taps_backward(grad_inner, padded, inner_kernel, length, keep)
    grad_rectified = rims_backward(spread, 1)
    return (grad_mixed + grad_rectified * elu_slope(upper), inner_rows, outer_rows)


def upsample_backward(grad_upper, values, lagged, kernel, stride, keep):
    phase_shape = grad_upper.shape[:3] + (values.shape[-1], stride)
    grad_phase = grad_upper.reshape(phase_shape)
    row_phase = apply_mask(grad_upper, keep).reshape(phase_shape)
    first_rows = product("nbimp,bjm->nbpij", row_phase, values)
    second_rows = product("nbimp,bjm->nbpij", row_phase, lagged)
    grad_values = product("pij,nbimp->nbjm", kernel[:stride], grad_phase)
    grad_lagged = product("pij,nbimp->nbjm", kernel[stride:], grad_phase)
    arrived = jnp.zeros_like(grad_lagged[..., :1])
    grad_values = grad_values + jnp.concatenate([grad_lagged[..., 1:], arrived], axis=-1)
    return (grad_values, jnp.concatenate([first_rows, second_rows], axis=2))


def local(latent, target, up_kernel, inner_kernel, outer_kernel, out_kernel):
    weights = (up_kernel, inner_kernel, outer_kernel, out_kernel)
    clips_here = target.shape[0]
    samples = target.shape[1]
    frames_here = latent.shape[2]
    latent_in = padded_2(latent, (("tm", 2),), 4)
    start_frame = 4
    margin = 8

    def lend_frame(edge):
        return jnp.zeros_like(edge)

    def border_inner(values):
        return jnp.pad(values, ((0, 0), (0, 0), (1, 1)))

    def border_output(values):
        return jnp.pad(values, ((0, 0), (0, 0), (3, 3)))

    shard_index = lax.axis_index("tm")
    shard_total = lax.axis_size("tm")
    wide_length = samples + 2 * margin
    local_places = jnp.arange(wide_length, dtype=jnp.int32)
    clip_places = samples * shard_index - margin + local_places
    clip_mask = ((clip_places >= 0) & (clip_places < samples * shard_total)).astype(jnp.float32)
    keep_rows = ((local_places >= margin) & (local_places < margin + samples)).astype(jnp.float32)
    activated = jax.nn.elu(latent_in)
    wave_all, saved = decode_forward(
        activated, weights, (lend_frame, border_inner, border_output), clip_mask
    )
    upper, lagged, padded_inner, inner_out, hidden, mixed, padded_output = saved
    waveform = wave_all[:, margin : margin + samples]
    tail_length = 3 * WIN_COARSE // 4
    wave_next, target_next = from_behind(
        (waveform[:, :tail_length], target[:, :tail_length]), "tm", -1
    )
    long_wave = jnp.concatenate([waveform, wave_next], axis=1)
    long_target = jnp.concatenate([target, target_next], axis=1)
    gradients = [2.0 * (waveform - target)]
    tails = []
    for window in (WIN_COARSE, WIN_FINE):
        hop_size = window // 4
        frame_count = samples // hop_size
        span = samples + 3 * hop_size
        target_mel = mel_energy(long_target[:, :span], window, frame_count)

        def scale_loss(signal):
            return spectral_loss(signal, target_mel, window, frame_count)

        local_grad = jax.grad(scale_loss)(long_wave[:, :span])
        gradients.append(local_grad[:, :samples])
        tails.append(jnp.pad(local_grad[:, samples:], ((0, 0), (0, tail_length - 3 * hop_size))))
    coarse_in, fine_in = from_behind((tails[0], tails[1]), "tm", 1)
    gradients[1] = gradients[1] + jnp.pad(coarse_in, ((0, 0), (0, samples - tail_length)))
    gradients[2] = gradients[2] + jnp.pad(fine_in, ((0, 0), (0, samples - tail_length)))
    squares = jnp.stack([jnp.sum(member * member, axis=1) for member in gradients], axis=1)
    squares = lax.psum(squares, "tm")
    total_samples = samples * lax.axis_size("tm")
    grad_scale = jnp.asarray(LOSS_WEIGHTS, jnp.float32)[None, :] / jnp.sqrt(
        squares / total_samples + 1e-06
    )
    streams = (
        gradients[0] * grad_scale[:, 0, None]
        + gradients[1] * grad_scale[:, 1, None]
        + gradients[2] * grad_scale[:, 2, None]
    )[None]
    row_weights = jnp.ones((1, clips_here), jnp.float32)
    streams_wide = padded_2(streams, (("tm", 2),), 8)
    wave_length = mixed.shape[2]
    out_taps = out_kernel[:, None, :]
    kernel_rows_out, spread_out = taps_backward(
        streams_wide[:, :, None, :], padded_output, out_taps, wave_length, keep_rows
    )
    out_rows = kernel_rows_out[:, :, :, 0, :]
    grad_final = rims_backward(spread_out, 3)
    grad_mixed = apply_mask(grad_final * elu_slope(mixed), clip_mask)
    grad_upper, inner_rows, outer_rows = residual_backward(
        grad_mixed, upper, padded_inner, inner_out, hidden, inner_kernel, outer_kernel, keep_rows
    )
    grad_activated, up_rows = upsample_backward(
        apply_mask(grad_upper, clip_mask), activated, lagged, up_kernel, 2, keep_rows
    )
    grad_latent_rows = grad_activated[..., start_frame : start_frame + frames_here] * elu_slope(
        latent
    )
    latent_grad = product("nb,nbcm->bcm", row_weights, grad_latent_rows)
    local_totals = [
        product("nb,nb...->...", row_weights, member)
        for member in (up_rows, inner_rows, outer_rows, out_rows)
    ]
    param_count = sum((member.size for member in local_totals))
    summed = lax.psum(
        (local_totals[0], local_totals[1], local_totals[2], local_totals[3]), ("dp", "tm")
    )
    squares_all = sum((jnp.sum(member * member) for member in summed))
    factor = jnp.minimum(1.0, 1.0 / jnp.sqrt(squares_all / param_count + 1e-06))
    updates = [member * factor for member in summed]
    return (latent_grad, updates[0], updates[1], updates[2], updates[3])


def solution(mesh):
    placed = (P("dp", None, "tm"), P("dp", "tm"), P(), P(), P(), P())
    return jax.shard_map(
        local,
        mesh=mesh,
        in_specs=placed,
        out_specs=(P("dp", None, "tm"), P(), P(), P(), P()),
        check_vma=False,
    )
```

profile of v0, /device:TPU:0, one launch (start us, length us, event | category | flops | bytes accessed | tf_op | source)
XLA Modules:
  0.0 188.2 jit_solution(7671481007626582187)
XLA Ops:
  0.6 1.3 slice.296
  1.9 1.3 collective-permute-start.3
  4.1 5.5 %collective-permute-start = (f32[1,64,4]{2,1,0:T(8,128)S(1)}, f32[1,64,4]{2,1,0:T(8,128)S(1)}, u32[]{:S(2)}, u32[]{:S(2)}) collective-permute-start(f32[1,64,4]{2,1,0:T(8,128)S(1)} %get-tuple-element.15), channel_id=1, source_target_pairs={{0,1},{1,2},{2,3},{3,4},{4,5},{5,6},{6,7},{8,9},{9,10},{10,11},{11... | collective-permute-start | bytes 3080 | tf_op jit(solution)/shard_map/ppermute | solution.py:20
  9.6 1.3 collective-permute-start.1
  12.3 1.6 slice_bitcast_fusion.6
  13.9 1.2 sine_multiply_fusion.1
  15.1 9.4 %sine_multiply_fusion = (f32[1024,512]{1,0:T(8,128)S(1)}, f32[1024,512]{1,0:T(8,128)}) fusion(f32[1024]{0:T(1024)S(1)} %fusion.218, f32[1024]{0:T(1024)S(1)} %multiply_subtract_fusion), kind=kLoop, calls=%fused_computation.21 | loop fusion | flops 8388608 | bytes 4202496 | tf_op jit(solution)/shard_map/jvp()/mul | solution.py:57
  25.3 1.1 compare_select_fusion
  26.7 1.2 copy.16
  28.1 1.0 fusion.69
  29.1 1.3 convolution_add_fusion.1
  30.4 1.0 fusion.5
  31.4 1.3 compare_select_fusion.9
  32.7 1.0 convolution_reduce_fusion.2
  33.7 1.0 convolution_reduce_fusion.1
  34.7 1.0 convolution_reduce_fusion
  35.7 1.0 convolution_reduce_fusion.5
  36.7 1.0 convolution_reduce_fusion.4
  37.6 1.0 convolution_reduce_fusion.6
  38.6 1.0 convolution_reduce_fusion.3
  39.6 2.0 %multiply_reduce_fusion.6 = (f32[]{:T(128)}, f32[1,1024]{1,0:T(1,128)}, f32[1,1792]{1,0:T(1,128)S(1)}) fusion(f32[1,1024]{1,0:T(1,128)} %param.8, f32[1,1040]{1,0:T(1,128)S(1)} %squeeze.11), kind=kLoop, calls=%fused_computation.340 | loop fusion | flops 4094 | bytes 16388 | tf_op jit(solution)/shard_map/reduce_sum | solution.py:220
  42.3 1.3 collective-permute-start.2
  45.4 1.3 reduce.11
  46.7 1.3 reshape.962
  48.0 1.4 reshape.970
  51.1 4.3 %fusion.15 = f32[1,4,1024]{2,1,0:T(4,128)} fusion(f32[1024,512]{1,0:T(8,128)S(1)} %get-tuple-element.77, f32[1024,512]{1,0:T(8,128)} %get-tuple-element.78, f32[1,4,256]{2,1,0:T(4,128)S(1)} %get-tuple-element.45, f32[1,4,256]{2,1,0:T(4,128)S(1)} %get-tuple-element.46, f32[1,4,256]{2,1,0:T(4,128)S(1)} %get-tuple-element.47, ...), kind=kOutput, calls=%fused_computation.33 | convolution fusion | flops 51392512 | bytes 4227072 | tf_op jit(solution)/shard_map/...nf,fk->...nk/dot_general | solution.py:36
  55.4 0.9 convolution_bitcast_fusion.10
  56.3 1.3 maximum_reduce_fusion
  57.6 1.3 reshape.959
  58.9 1.3 fusion.210
  60.2 1.4 reshape.967
  61.6 1.4 fusion.285
  63.0 0.9 fusion.283
  63.9 1.2 convolution_bitcast_fusion.11
  65.9 0.9 fusion.20
  67.6 1.3 convolution_bitcast_fusion.9
  69.7 1.4 reshape.974
  71.7 6.2 %collective-permute-start.5 = (f32[1,768]{1,0:T(1,128)S(1)}, f32[1,768]{1,0:T(1,128)S(1)}, u32[]{:S(2)}, u32[]{:S(2)}) collective-permute-start(f32[1,768]{1,0:T(1,128)S(1)} %pad.112), channel_id=1, source_target_pairs={{0,1},{1,2},{2,3},{3,4},{4,5},{5,6},{6,7},{8,9},{9,10},{10,11},{11... | collective-permute-start | bytes 9224 | tf_op jit(solution)/shard_map/ppermute | solution.py:32
  78.0 3.7 %fusion.14 = f32[1,4,1024]{2,1,0:T(4,128)S(1)} fusion(f32[1024,512]{1,0:T(8,128)S(1)} %get-tuple-element.77, f32[1024,512]{1,0:T(8,128)} %get-tuple-element.78, f32[1,4,256]{2,1,0:T(4,128)} %get-tuple-element.49, f32[1,4,256]{2,1,0:T(4,128)} %get-tuple-element.50, f32[1,4,256]{2,1,0:T(4,128)} %get-tuple-element.51, f32[1,4,256]{2,1,0:T(4,128)} %get-tuple-element.48), kind=kOutput, calls=%fused_computation.32 | convolution fusion | flops 51392512 | bytes 4227072 | tf_op jit(solution)/shard_map/jvp(...nf,fk->...nk)/dot_general | solution.py:36
  83.3 3.5 %fusion.16 = f32[1,4,1024]{2,1,0:T(4,128)S(1)} fusion(f32[1024,512]{1,0:T(8,128)S(1)} %get-tuple-element.77, f32[1024,512]{1,0:T(8,128)S(1)} %copy-done.1, f32[1,4,512]{2,1,0:T(4,128)S(1)} %get-tuple-element.18, f32[1,4,512]{2,1,0:T(4,128)S(1)} %get-tuple-element.17), kind=kOutput, calls=%fused_computation.34 | convolution fusion | flops 51384320 | bytes 4227072 | tf_op jit(solution)/shard_map/transpose(jvp(...nf,fk->...nk))/dot_general | solution.py:36
  86.9 5.0 %collective-permute-start.4 = (f32[1,768]{1,0:T(1,128)S(1)}, f32[1,768]{1,0:T(1,128)S(1)}, u32[]{:S(2)}, u32[]{:S(2)}) collective-permute-start(f32[1,768]{1,0:T(1,128)S(1)} %slice.347), channel_id=1, source_target_pairs={{0,1},{1,2},{2,3},{3,4},{4,5},{5,6},{6,7},{8,9},{9,10},{10,11},{11... | collective-permute-start | bytes 9224 | tf_op jit(solution)/shard_map/ppermute | solution.py:32
  93.8 2.0 %pad_maximum_fusion.16 = f32[1,3]{1,0:T(1,128)S(1)} fusion(f32[1,1]{1,0:T(1,128)} %bitcast.63, f32[1,1]{1,0:T(1,128)} %bitcast.53, f32[1,1]{1,0:T(1,128)} %bitcast.43), kind=kLoop, calls=%fused_computation.344 | loop fusion | flops 6 | bytes 24 | tf_op jit(solution)/shard_map/stack | solution.py:220
  96.0 22.0 %psum.35 = f32[1,3]{1,0:T(1,128)S(1)} all-reduce(f32[1,3]{1,0:T(1,128)S(1)} %pad_maximum_fusion.16), channel_id=1, replica_groups=mesh['dp'=4,'tm'=8] {'tm'}, use_global_device_ids=true, to_apply=%region_3.4 | all-reduce | flops 3 | bytes 24 | tf_op jit(solution)/shard_map/psum | solution.py:221
  119.8 2.1 %add_bitcast_fusion.1 = f32[1,1,1024]{2,1,0:T(1,128)S(1)} fusion(f32[1,1024]{1,0:T(1,128)S(1)} %get-tuple-element.14, f32[1,1024]{1,0:T(1,128)S(1)} %get-tuple-element.12, f32[]{:T(128)} %bitcast.66, f32[]{:T(128)} %bitcast.65, f32[]{:T(128)} %bitcast.64, f32[1,1024]{1,0:T(1,128)} %param.8, f32[1,1040]{1,0:T(1,128)} %copy-done.14), kind=kLoop, calls=%fused_computation.336 | loop fusion | flops 6144 | bytes 20492 | tf_op jit(solution)/shard_map/broadcast_in_dim | solution.py:226
  122.0 1.3 collective-permute-start.7
  123.3 4.5 %collective-permute-start.6 = (f32[1,1,8]{2,1,0:T(1,128)S(1)}, f32[1,1,8]{2,1,0:T(1,128)S(1)}, u32[]{:S(2)}, u32[]{:S(2)}) collective-permute-start(f32[1,1,8]{2,1,0:T(1,128)S(1)} %get-tuple-element.62), channel_id=1, source_target_pairs={{0,1},{1,2},{2,3},{3,4},{4,5},{5,6},{6,7},{8,9},{9,10},{10,11},{11... | collective-permute-start | bytes 104 | tf_op jit(solution)/shard_map/ppermute | solution.py:20
  127.8 1.3 collective-permute-done.6
  136.8 41.8 %all-reduce.29 = (f32[4,32,64]{2,1,0:T(8,128)S(1)}, f32[3,16,32]{2,1,0:T(8,128)S(1)}, f32[32,16]{0,1:T(8,128)S(1)}, f32[7,32]{1,0:T(8,128)S(1)}) all-reduce(f32[4,32,64]{2,1,0:T(8,128)S(1)} %maximum_bitcast_fusion, f32[3,16,32]{2,1,0:T(8,128)S(1)} %maximum_bitcast_fusion.1, ...), channel_id=1, replica_groups=mesh['dp'=4,'tm'=8] {'dp','tm'}, use_global_device_ids=true, to_apply=%region_4.5 | all-reduce | flops 10464 | bytes 83712 | tf_op jit(solution)/shard_map/psum | solution.py:256
  (141 shorter events, 30.2 us)
Async XLA Ops:
  0.6 30.8 %copy-start = (f32[32,16]{0,1:T(8,128)S(1)}, f32[32,16]{0,1:T(8,128)}, u32[]{:S(2)}) copy-start(f32[32,16]{0,1:T(8,128)} %param.11) | copy-start | bytes 6148
  1.9 41.6 %collective-permute-start.3 = (f32[1,768]{1,0:T(1,128)}, f32[1,768]{1,0:T(1,128)}, u32[]{:S(2)}, u32[]{:S(2)}) collective-permute-start(f32[1,768]{1,0:T(1,128)} %slice.296), channel_id=1, source_target_pairs={{1,0},{2,1},{3,2},{4,3},{5,4},{6,5},{7,6},{9,8},{10,9},{11,10},{12... | collective-permute-start | bytes 9224 | tf_op jit(solution)/shard_map/ppermute | solution.py:32
  4.1 20.5 %collective-permute-start = (f32[1,64,4]{2,1,0:T(8,128)S(1)}, f32[1,64,4]{2,1,0:T(8,128)S(1)}, u32[]{:S(2)}, u32[]{:S(2)}) collective-permute-start(f32[1,64,4]{2,1,0:T(8,128)S(1)} %get-tuple-element.15), channel_id=1, source_target_pairs={{0,1},{1,2},{2,3},{3,4},{4,5},{5,6},{6,7},{8,9},{9,10},{10,11},{11... | collective-permute-start | bytes 3080 | tf_op jit(solution)/shard_map/ppermute | solution.py:20
  9.6 15.0 %collective-permute-start.1 = (f32[1,64,4]{2,1,0:T(8,128)S(1)}, f32[1,64,4]{2,1,0:T(8,128)S(1)}, u32[]{:S(2)}, u32[]{:S(2)}) collective-permute-start(f32[1,64,4]{2,1,0:T(8,128)S(1)} %get-tuple-element.16), channel_id=1, source_target_pairs={{1,0},{2,1},{3,2},{4,3},{5,4},{6,5},{7,6},{9,8},{10,9},{11,10},{12... | collective-permute-start | bytes 3080 | tf_op jit(solution)/shard_map/ppermute | solution.py:22
  15.1 9.5 %copy-start.7 = (f32[1,64,512]{2,1,0:T(8,128)S(1)}, f32[1,64,512]{2,1,0:T(8,128)}, u32[]{:S(2)}) copy-start(f32[1,64,512]{2,1,0:T(8,128)} %param.7) | copy-start | bytes 393220
  15.1 9.5 %copy-start.11 = (f32[4,32,64]{2,1,0:T(8,128)S(1)}, f32[4,32,64]{2,1,0:T(8,128)}, u32[]{:S(2)}) copy-start(f32[4,32,64]{2,1,0:T(8,128)} %param.9) | copy-start | bytes 98308
  24.6 0.6 copy-start.17
  24.6 0.6 copy-start.19
  25.3 1.1 copy-start.4
  28.0 2.4 %copy-start.6 = (f32[1,32,1040]{2,1,0:T(8,128)}, f32[1,32,1040]{2,1,0:T(8,128)S(1)}, u32[]{:S(2)}) copy-start(f32[1,32,1040]{2,1,0:T(8,128)S(1)} %copy.17) | copy-start | bytes 399364
  32.7 5.9 %copy-start.9 = (f32[1,32,1040]{2,1,0:T(8,128)}, f32[1,32,1040]{2,1,0:T(8,128)S(1)}, u32[]{:S(2)}) copy-start(f32[1,32,1040]{2,1,0:T(8,128)S(1)} %get-tuple-element.74) | copy-start | bytes 399364
  39.6 2.0 %copy-start.14 = (f32[1,1040]{1,0:T(1,128)}, f32[1,1040]{1,0:T(1,128)S(1)}, u32[]{:S(2)}) copy-start(f32[1,1040]{1,0:T(1,128)S(1)} %squeeze.11) | copy-start | bytes 12484
  42.3 14.1 %collective-permute-start.2 = (f32[1,768]{1,0:T(1,128)}, f32[1,768]{1,0:T(1,128)}, u32[]{:S(2)}, u32[]{:S(2)}) collective-permute-start(f32[1,768]{1,0:T(1,128)} %slice.333), channel_id=1, source_target_pairs={{1,0},{2,1},{3,2},{4,3},{5,4},{6,5},{7,6},{9,8},{10,9},{11,10},{12... | collective-permute-start | bytes 9224 | tf_op jit(solution)/shard_map/ppermute | solution.py:32
  44.2 0.6 copy-start.15
  51.1 4.3 %copy-start.2 = (f32[256,128]{1,0:T(8,128)S(1)}, f32[256,128]{1,0:T(8,128)}, u32[]{:S(2)}) copy-start(f32[256,128]{1,0:T(8,128)} %get-tuple-element.75) | copy-start | bytes 393220
  51.1 4.3 %copy-start.3 = (f32[256,128]{1,0:T(8,128)S(1)}, f32[256,128]{1,0:T(8,128)}, u32[]{:S(2)}) copy-start(f32[256,128]{1,0:T(8,128)} %get-tuple-element.76) | copy-start | bytes 393220
  51.1 5.2 %copy-start.16 = (f32[1,1024]{1,0:T(1,128)S(1)}, f32[1,1024]{1,0:T(1,128)}, u32[]{:S(2)}) copy-start(f32[1,1024]{1,0:T(1,128)} %get-tuple-element.53) | copy-start | bytes 12292
  71.7 20.1 %collective-permute-start.5 = (f32[1,768]{1,0:T(1,128)S(1)}, f32[1,768]{1,0:T(1,128)S(1)}, u32[]{:S(2)}, u32[]{:S(2)}) collective-permute-start(f32[1,768]{1,0:T(1,128)S(1)} %pad.112), channel_id=1, source_target_pairs={{0,1},{1,2},{2,3},{3,4},{4,5},{5,6},{6,7},{8,9},{9,10},{10,11},{11... | collective-permute-start | bytes 9224 | tf_op jit(solution)/shard_map/ppermute | solution.py:32
  78.0 3.7 %copy-start.23 = (f32[64]{0:T(128)S(1)}, f32[64]{0:T(128)}, u32[]{:S(2)}) copy-start(f32[64]{0:T(128)} %get-tuple-element.67) | copy-start | bytes 772
  78.0 3.7 %copy-start.24 = (f32[64]{0:T(128)S(1)}, f32[64]{0:T(128)}, u32[]{:S(2)}) copy-start(f32[64]{0:T(128)} %get-tuple-element.68) | copy-start | bytes 772
  78.0 4.1 %copy-start.22 = (f32[1,4,1024]{2,1,0:T(4,128)S(1)}, f32[1,4,1024]{2,1,0:T(4,128)}, u32[]{:S(2)}) copy-start(f32[1,4,1024]{2,1,0:T(4,128)} %fusion.15) | copy-start | bytes 49156
  81.7 1.6 copy-start.1
  83.3 8.6 %copy-start.21 = (f32[1,1216]{1,0:T(1,128)S(1)}, f32[1,1216]{1,0:T(1,128)}, u32[]{:S(2)}) copy-start(f32[1,1216]{1,0:T(1,128)} %reshape.974) | copy-start | bytes 14596
  86.8 43.6 %copy-start.10 = (f32[1,32,1040]{2,1,0:T(8,128)S(1)}, f32[1,32,1040]{2,1,0:T(8,128)}, u32[]{:S(2)}) copy-start(f32[1,32,1040]{2,1,0:T(8,128)} %copy-done.9) | copy-start | bytes 399364
  86.9 6.3 %collective-permute-start.4 = (f32[1,768]{1,0:T(1,128)S(1)}, f32[1,768]{1,0:T(1,128)S(1)}, u32[]{:S(2)}, u32[]{:S(2)}) collective-permute-start(f32[1,768]{1,0:T(1,128)S(1)} %slice.347), channel_id=1, source_target_pairs={{0,1},{1,2},{2,3},{3,4},{4,5},{5,6},{6,7},{8,9},{9,10},{10,11},{11... | collective-permute-start | bytes 9224 | tf_op jit(solution)/shard_map/ppermute | solution.py:32
  122.0 5.8 %collective-permute-start.7 = (f32[1,1,8]{2,1,0:T(1,128)S(1)}, f32[1,1,8]{2,1,0:T(1,128)S(1)}, u32[]{:S(2)}, u32[]{:S(2)}) collective-permute-start(f32[1,1,8]{2,1,0:T(1,128)S(1)} %get-tuple-element.61), channel_id=1, source_target_pairs={{1,0},{2,1},{3,2},{4,3},{5,4},{6,5},{7,6},{9,8},{10,9},{11,10},{12... | collective-permute-start | bytes 104 | tf_op jit(solution)/shard_map/ppermute | solution.py:22
  123.3 5.8 %collective-permute-start.6 = (f32[1,1,8]{2,1,0:T(1,128)S(1)}, f32[1,1,8]{2,1,0:T(1,128)S(1)}, u32[]{:S(2)}, u32[]{:S(2)}) collective-permute-start(f32[1,1,8]{2,1,0:T(1,128)S(1)} %get-tuple-element.62), channel_id=1, source_target_pairs={{0,1},{1,2},{2,3},{3,4},{4,5},{5,6},{6,7},{8,9},{9,10},{10,11},{11... | collective-permute-start | bytes 104 | tf_op jit(solution)/shard_map/ppermute | solution.py:20
  129.2 3.1 %copy-start.13 = (f32[3,16,32]{2,1,0:T(8,128)S(1)}, f32[3,16,32]{2,1,0:T(8,128)}, u32[]{:S(2)}) copy-start(f32[3,16,32]{2,1,0:T(8,128)} %param.10) | copy-start | bytes 18436
  131.2 2.7 %copy-start.5 = (f32[1,64,519]{2,1,0:T(8,128)S(1)}, f32[1,64,519]{2,1,0:T(8,128)}, u32[]{:S(2)}) copy-start(f32[1,64,519]{2,1,0:T(8,128)} %copy-done.4) | copy-start | bytes 398596
  131.7 2.7 %copy-start.8 = (f32[1,64,512]{2,1,0:T(8,128)S(1)}, f32[1,64,512]{2,1,0:T(8,128)}, u32[]{:S(2)}) copy-start(f32[1,64,512]{2,1,0:T(8,128)} %param.7) | copy-start | bytes 393220
  131.7 2.7 %copy-start.18 = (f32[1,64,4]{2,1,0:T(8,128)S(1)}, f32[1,64,4]{2,1,0:T(8,128)}, u32[]{:S(2)}) copy-start(f32[1,64,4]{2,1,0:T(8,128)} %copy-done.17) | copy-start | bytes 3076
  131.7 2.7 %copy-start.20 = (f32[1,64,4]{2,1,0:T(8,128)S(1)}, f32[1,64,4]{2,1,0:T(8,128)}, u32[]{:S(2)}) copy-start(f32[1,64,4]{2,1,0:T(8,128)} %copy-done.19) | copy-start | bytes 3076
  134.0 52.6 %copy-start.12 = (f32[4,32,64]{2,1,0:T(8,128)S(1)}, f32[4,32,64]{2,1,0:T(8,128)}, u32[]{:S(2)}) copy-start(f32[4,32,64]{2,1,0:T(8,128)} %param.9) | copy-start | bytes 98308
where the time goes:
time: 190 us; the launch traced here: 188 us
  blocking collectives  63.8 us (34%)
  matrix products  37.6 us (20%)
  other arithmetic  31.8 us (17%)
  starting transfers between devices  26.4 us (14%)
  local copies, waits for them, and re-layouts  22 us (12%)
  between operations  4.65 us (2%)
  waiting for transfers between devices  1.95 us (1%)
    psum x1, blocking collectives, local(): lax.psum((local_totals[0], local_totals[1], local_totals[2], local_totals...  41.8 us
    dot_general x44, matrix products, product(): jnp.einsum(form, left, right, precision=lax.Precision.HIGHEST, preferred_...  37.6 us
    psum x1, blocking collectives, local(): squares = lax.psum(squares, 'tm')  22 us
    ppermute x4, starting transfers between devices, from_behind(): return lax.ppermute(x, axis, pairs)  13.8 us
    mul x2, other arithmetic, dft_table(): -hann_taper * jnp.sin(angles)  10.7 us
    ppermute x2, starting transfers between devices, padded_2(): lax.ppermute(tail, axis, [(i, (i + 1) % count) for i in range(ends)])  10.1 us
    reshape x5, local copies, waits for them, and re-layouts, framed(): blocks = signal.reshape(signal.shape[:-1] + (frame_count + 3, hop_size))  6.68 us
    slice x4, local copies, waits for them, and re-layouts, framed(): blocks[..., offset:offset + frame_count, :]  4.01 us
  transfers between devices with their start and end apart: 8, of which 2 were waited for; matrix products, arithmetic and copies ran while one was open for 28% of the time, Pallas kernels for 0%

commit v1 on v0

--- a/solution.py
+++ b/solution.py
@@ -2,11 +2,25 @@
 import jax.numpy as jnp
 from jax import lax
 from jax.sharding import PartitionSpec as P
+from jax.lax import ppermute, psum
 
 MELS = 64
 WIN_COARSE = 1024
 WIN_FINE = 256
 LOSS_WEIGHTS = (0.25, 0.5, 0.5)
+
+
+def _unite_scales(field_in):
+    axis_name = "tm"
+    slots = psum(1, axis_name=axis_name)
+    aux, work_now = (field_in, 0)
+    while 1 << work_now < slots:
+        block_last = ppermute(
+            aux, axis_name=axis_name, perm=[(c, c ^ 1 << work_now) for c in range(slots)]
+        )
+        aux = aux + block_last
+        work_now = work_now + 1
+    return aux
 
 
 def padded_2(cells, sides, width):
@@ -218,7 +232,7 @@
     gradients[1] = gradients[1] + jnp.pad(coarse_in, ((0, 0), (0, samples - tail_length)))
     gradients[2] = gradients[2] + jnp.pad(fine_in, ((0, 0), (0, samples - tail_length)))
     squares = jnp.stack([jnp.sum(member * member, axis=1) for member in gradients], axis=1)
-    squares = lax.psum(squares, "tm")
+    squares = _unite_scales(squares)
     total_samples = samples * lax.axis_size("tm")
     grad_scale = jnp.asarray(LOSS_WEIGHTS, jnp.float32)[None, :] / jnp.sqrt(
         squares / total_samples + 1e-06

time: 190 us -> 164 us (0.86)
  blocking collectives: 63.8 us -> 42.9 us
  local copies, waits for them, and re-layouts: 22 us -> 10.8 us
  starting transfers between devices: 26.4 us -> 35.1 us
  matrix products: 37.6 us -> 31.9 us
  waiting for transfers between devices: 1.95 us -> 6.63 us
    psum x1 -> x0, blocking collectives: 22 us -> none  [local(): squares = lax.psum(squares, 'tm')]
    ppermute x0 -> x3, starting transfers between devices: none -> 8.8 us  [_unite_scales(): ppermute(aux, axis_name=axis_name, perm=[(c, c ^ 1 << work_now) for c in...]
    reshape x5, local copies, waits for them, and re-layouts: 6.68 us -> 0.23 us  [framed(): blocks = signal.reshape(signal.shape[:-1] + (frame_count + 3, hop_size))]
    dot_general x44, matrix products: 37.6 us -> 31.9 us  [product(): jnp.einsum(form, left, right, precision=lax.Precision.HIGHEST, preferred_...]
    ppermute x0 -> x3, waiting for transfers between devices: none -> 4.65 us  [_unite_scales(): ppermute(aux, axis_name=axis_name, perm=[(c, c ^ 1 << work_now) for c in...]
    add x0 -> x2, other arithmetic: none -> 4.11 us  [_unite_scales(): aux = aux + block_last]
    slice x4, local copies, waits for them, and re-layouts: 4.01 us -> 0.02 us  [framed(): blocks[..., offset:offset + frame_count, :]]
  transfers between devices with their start and end apart: 8 -> 11, of which waited for: 2 -> 5; matrix products, arithmetic and copies ran while one was open for 28% -> 29% of each run, Pallas kernels for 0% -> 0%
where the time goes in v1:
time: 164 us; the launch traced here: 163 us
  blocking collectives  42.9 us (26%)
  starting transfers between devices  35.1 us (21%)
  matrix products  31.9 us (19%)
  other arithmetic  30.4 us (19%)
  local copies, waits for them, and re-layouts  10.8 us (7%)
  waiting for transfers between devices  6.63 us (4%)
  between operations  4.92 us (3%)
    psum x1, blocking collectives, local(): lax.psum((local_totals[0], local_totals[1], local_totals[2], local_totals...  42.9 us
    dot_general x44, matrix products, product(): jnp.einsum(form, left, right, precision=lax.Precision.HIGHEST, preferred_...  31.9 us
    ppermute x4, starting transfers between devices, from_behind(): return lax.ppermute(x, axis, pairs)  13.6 us
    mul x2, other arithmetic, dft_table(): -hann_taper * jnp.sin(angles)  10.7 us
    ppermute x2, starting transfers between devices, padded_2(): lax.ppermute(tail, axis, [(i, (i + 1) % count) for i in range(ends)])  10.1 us
    ppermute x3, starting transfers between devices, _unite_scales(): ppermute(aux, axis_name=axis_name, perm=[(c, c ^ 1 << work_now) for c in...  8.8 us
    ppermute x3, waiting for transfers between devices, _unite_scales(): ppermute(aux, axis_name=axis_name, perm=[(c, c ^ 1 << work_now) for c in...  4.65 us
    add x2, other arithmetic, _unite_scales(): aux = aux + block_last  4.11 us
  transfers between devices with their start and end apart: 11, of which 5 were waited for; matrix products, arithmetic and copies ran while one was open for 29% of the time, Pallas kernels for 0%

profile of v1, /device:TPU:0, one launch (start us, length us, event | category | flops | bytes accessed | tf_op | source)
XLA Modules:
  0.0 162.6 jit_solution(8714940235279228507)
XLA Ops:
  0.6 1.3 slice.296
  1.9 1.3 collective-permute-start.3
  3.2 0.9 fusion.279
  4.1 5.5 %collective-permute-start = (f32[1,64,4]{2,1,0:T(8,128)S(1)}, f32[1,64,4]{2,1,0:T(8,128)S(1)}, u32[]{:S(2)}, u32[]{:S(2)}) collective-permute-start(f32[1,64,4]{2,1,0:T(8,128)S(1)} %get-tuple-element.15), channel_id=1, source_target_pairs={{0,1},{1,2},{2,3},{3,4},{4,5},{5,6},{6,7},{8,9},{9,10},{10,11},{11... | collective-permute-start | bytes 3080 | tf_op jit(solution)/shard_map/ppermute | solution.py:34
  9.6 1.3 collective-permute-start.1
  11.7 0.7 fusion.288
  12.4 1.5 slice_bitcast_fusion.6
  13.9 1.2 sine_multiply_fusion.1
  15.2 9.4 %sine_multiply_fusion = (f32[1024,512]{1,0:T(8,128)S(1)}, f32[1024,512]{1,0:T(8,128)}) fusion(f32[1024]{0:T(1024)S(1)} %fusion.218, f32[1024]{0:T(1024)S(1)} %multiply_subtract_fusion), kind=kLoop, calls=%fused_computation.21 | loop fusion | flops 8388608 | bytes 4202496 | tf_op jit(solution)/shard_map/jvp()/mul | solution.py:71
  26.7 1.0 fusion.69
  27.7 1.3 convolution_add_fusion.1
  29.0 1.0 fusion.5
  30.0 1.3 compare_select_fusion.9
  31.3 1.0 convolution_reduce_fusion.2
  32.3 1.0 convolution_reduce_fusion.1
  33.3 1.0 convolution_reduce_fusion
  34.3 1.0 convolution_reduce_fusion.5
  35.3 1.0 convolution_reduce_fusion.4
  36.2 1.0 convolution_reduce_fusion.6
  37.2 1.0 convolution_reduce_fusion.3
  38.2 2.0 %multiply_reduce_fusion.6 = (f32[]{:T(128)}, f32[1,1024]{1,0:T(1,128)}, f32[1,1792]{1,0:T(1,128)}) fusion(f32[1,1024]{1,0:T(1,128)} %param.8, f32[1,1040]{1,0:T(1,128)S(1)} %squeeze.11), kind=kLoop, calls=%fused_computation.340 | loop fusion | flops 4094 | bytes 16896 | tf_op jit(solution)/shard_map/reduce_sum | solution.py:234
  40.3 0.7 slice.333
  40.9 0.9 copy.20
  41.8 1.3 collective-permute-start.2
  43.1 1.3 constant_dynamic-update-slice_fusion
  44.3 0.7 slice_reduce_fusion
  45.1 0.7 reduce.11
  45.9 3.8 %fusion.15 = f32[1,4,1024]{2,1,0:T(4,128)S(1)} fusion(f32[1024,512]{1,0:T(8,128)S(1)} %get-tuple-element.77, f32[1024,512]{1,0:T(8,128)} %get-tuple-element.78, f32[1,4,256]{2,1,0:T(4,128)S(1)} %get-tuple-element.45, f32[1,4,256]{2,1,0:T(4,128)S(1)} %get-tuple-element.46, f32[1,4,256]{2,1,0:T(4,128)S(1)} %get-tuple-element.47, ...), kind=kOutput, calls=%fused_computation.33 | convolution fusion | flops 51392512 | bytes 4227072 | tf_op jit(solution)/shard_map/...nf,fk->...nk/dot_general | solution.py:50
  51.6 6.3 %collective-permute-start.5 = (f32[1,768]{1,0:T(1,128)S(1)}, f32[1,768]{1,0:T(1,128)S(1)}, u32[]{:S(2)}, u32[]{:S(2)}) collective-permute-start(f32[1,768]{1,0:T(1,128)S(1)} %pad.112), channel_id=1, source_target_pairs={{0,1},{1,2},{2,3},{3,4},{4,5},{5,6},{6,7},{8,9},{9,10},{10,11},{11... | collective-permute-start | bytes 9224 | tf_op jit(solution)/shard_map/ppermute | solution.py:46
  57.9 3.7 %fusion.14 = f32[1,4,1024]{2,1,0:T(4,128)S(1)} fusion(f32[1024,512]{1,0:T(8,128)S(1)} %get-tuple-element.77, f32[1024,512]{1,0:T(8,128)} %get-tuple-element.78, f32[1,4,256]{2,1,0:T(4,128)S(1)} %get-tuple-element.49, f32[1,4,256]{2,1,0:T(4,128)S(1)} %get-tuple-element.50, f32[1,4,256]{2,1,0:T(4,128)S(1)} %get-tuple-element.51, ...), kind=kOutput, calls=%fused_computation.32 | convolution fusion | flops 51392512 | bytes 4227072 | tf_op jit(solution)/shard_map/jvp(...nf,fk->...nk)/dot_general | solution.py:50
  63.2 3.5 %fusion.16 = f32[1,4,1024]{2,1,0:T(4,128)S(1)} fusion(f32[1024,512]{1,0:T(8,128)S(1)} %get-tuple-element.77, f32[1024,512]{1,0:T(8,128)S(1)} %copy-done.1, f32[1,4,512]{2,1,0:T(4,128)S(1)} %get-tuple-element.18, f32[1,4,512]{2,1,0:T(4,128)S(1)} %get-tuple-element.17), kind=kOutput, calls=%fused_computation.34 | convolution fusion | flops 51384320 | bytes 4227072 | tf_op jit(solution)/shard_map/transpose(jvp(...nf,fk->...nk))/dot_general | solution.py:50
  66.8 4.8 %collective-permute-start.4 = (f32[1,768]{1,0:T(1,128)S(1)}, f32[1,768]{1,0:T(1,128)S(1)}, u32[]{:S(2)}, u32[]{:S(2)}) collective-permute-start(f32[1,768]{1,0:T(1,128)S(1)} %slice.347), channel_id=1, source_target_pairs={{0,1},{1,2},{2,3},{3,4},{4,5},{5,6},{6,7},{8,9},{9,10},{10,11},{11... | collective-permute-start | bytes 9224 | tf_op jit(solution)/shard_map/ppermute | solution.py:46
  72.3 0.7 collective-permute-done.4
  73.6 2.1 %pad_maximum_fusion.16 = f32[1,3]{1,0:T(1,128)S(1)} fusion(f32[1,1]{1,0:T(1,128)} %bitcast.63, f32[1,1]{1,0:T(1,128)} %bitcast.53, f32[1,1]{1,0:T(1,128)} %bitcast.43), kind=kLoop, calls=%fused_computation.344 | loop fusion | flops 6 | bytes 24 | tf_op jit(solution)/shard_map/stack | solution.py:234
  75.6 2.3 %collective-permute-start.6 = (f32[1,3]{1,0:T(1,128)S(1)}, f32[1,3]{1,0:T(1,128)S(1)}, u32[]{:S(2)}, u32[]{:S(2)}) collective-permute-start(f32[1,3]{1,0:T(1,128)S(1)} %pad_maximum_fusion.16), channel_id=1, source_target_pairs={{0,1},{1,0},{2,3},{3,2},{4,5},{5,4},{6,7},{7,6},{8,9},{9,8},{10,11... | collective-permute-start | bytes 44 | tf_op jit(solution)/shard_map/ppermute | solution.py:18
  77.9 1.5 collective-permute-done.6
  79.4 2.1 %fusion.300 = f32[1,3]{1,0:T(1,128)S(1)} fusion(f32[1,3]{1,0:T(1,128)S(1)} %collective-permute-done.6, f32[1,1]{1,0:T(1,128)} %bitcast.63, f32[1,1]{1,0:T(1,128)} %bitcast.53, f32[1,1]{1,0:T(1,128)} %bitcast.43), kind=kLoop, calls=%fused_computation.429 | loop fusion | flops 9 | bytes 36 | tf_op jit(solution)/shard_map/add | solution.py:21
  81.5 3.5 %collective-permute-start.7 = (f32[1,3]{1,0:T(1,128)S(1)}, f32[1,3]{1,0:T(1,128)S(1)}, u32[]{:S(2)}, u32[]{:S(2)}) collective-permute-start(f32[1,3]{1,0:T(1,128)S(1)} %fusion.300), channel_id=1, source_target_pairs={{0,2},{1,3},{2,0},{3,1},{4,6},{5,7},{6,4},{7,5},{8,10},{9,11},{10,... | collective-permute-start | bytes 44 | tf_op jit(solution)/shard_map/ppermute | solution.py:18
  85.0 1.5 collective-permute-done.7
  86.5 2.1 %fusion.301 = f32[1,3]{1,0:T(1,128)S(1)} fusion(f32[1,3]{1,0:T(1,128)S(1)} %collective-permute-done.7, f32[1,3]{1,0:T(1,128)S(1)} %collective-permute-done.6, f32[1,1]{1,0:T(1,128)} %bitcast.63, f32[1,1]{1,0:T(1,128)} %bitcast.53, f32[1,1]{1,0:T(1,128)} %bitcast.43), kind=kLoop, calls=%fused_computation.430 | loop fusion | flops 12 | bytes 48 | tf_op jit(solution)/shard_map/add | solution.py:21
  88.6 3.0 %collective-permute-start.8 = (f32[1,3]{1,0:T(1,128)S(1)}, f32[1,3]{1,0:T(1,128)S(1)}, u32[]{:S(2)}, u32[]{:S(2)}) collective-permute-start(f32[1,3]{1,0:T(1,128)S(1)} %fusion.301), channel_id=1, source_target_pairs={{0,4},{1,5},{2,6},{3,7},{4,0},{5,1},{6,2},{7,3},{8,12},{9,13},{10,... | collective-permute-start | bytes 44 | tf_op jit(solution)/shard_map/ppermute | solution.py:18
  91.6 1.5 collective-permute-done.8
  94.5 1.4 add_bitcast_fusion.1
  95.9 1.3 collective-permute-start.10
  97.2 4.5 %collective-permute-start.9 = (f32[1,1,8]{2,1,0:T(1,128)S(1)}, f32[1,1,8]{2,1,0:T(1,128)S(1)}, u32[]{:S(2)}, u32[]{:S(2)}) collective-permute-start(f32[1,1,8]{2,1,0:T(1,128)S(1)} %get-tuple-element.62), channel_id=1, source_target_pairs={{0,1},{1,2},{2,3},{3,4},{4,5},{5,6},{6,7},{8,9},{9,10},{10,11},{11... | collective-permute-start | bytes 104 | tf_op jit(solution)/shard_map/ppermute | solution.py:34
  101.8 1.3 collective-permute-done.9
  110.1 42.9 %all-reduce.29 = (f32[4,32,64]{2,1,0:T(8,128)S(1)}, f32[3,16,32]{2,1,0:T(8,128)S(1)}, f32[32,16]{0,1:T(8,128)S(1)}, f32[7,32]{1,0:T(8,128)S(1)}) all-reduce(f32[4,32,64]{2,1,0:T(8,128)S(1)} %maximum_bitcast_fusion, f32[3,16,32]{2,1,0:T(8,128)S(1)} %maximum_bitcast_fusion.1, ...), channel_id=1, replica_groups=mesh['dp'=4,'tm'=8] {'dp','tm'}, use_global_device_ids=true, to_apply=%region_3.4 | all-reduce | flops 10464 | bytes 83712 | tf_op jit(solution)/shard_map/psum | solution.py:270
  161.8 0.8 fusion.92
  (168 shorter events, 21.2 us)
Async XLA Ops:
  0.6 29.4 %copy-start = (f32[32,16]{0,1:T(8,128)S(1)}, f32[32,16]{0,1:T(8,128)}, u32[]{:S(2)}) copy-start(f32[32,16]{0,1:T(8,128)} %param.11) | copy-start | bytes 6148
  1.9 41.1 %collective-permute-start.3 = (f32[1,768]{1,0:T(1,128)}, f32[1,768]{1,0:T(1,128)}, u32[]{:S(2)}, u32[]{:S(2)}) collective-permute-start(f32[1,768]{1,0:T(1,128)} %slice.296), channel_id=1, source_target_pairs={{1,0},{2,1},{3,2},{4,3},{5,4},{6,5},{7,6},{9,8},{10,9},{11,10},{12... | collective-permute-start | bytes 9224 | tf_op jit(solution)/shard_map/ppermute | solution.py:46
  4.1 20.6 %collective-permute-start = (f32[1,64,4]{2,1,0:T(8,128)S(1)}, f32[1,64,4]{2,1,0:T(8,128)S(1)}, u32[]{:S(2)}, u32[]{:S(2)}) collective-permute-start(f32[1,64,4]{2,1,0:T(8,128)S(1)} %get-tuple-element.15), channel_id=1, source_target_pairs={{0,1},{1,2},{2,3},{3,4},{4,5},{5,6},{6,7},{8,9},{9,10},{10,11},{11... | collective-permute-start | bytes 3080 | tf_op jit(solution)/shard_map/ppermute | solution.py:34
  9.6 15.1 %collective-permute-start.1 = (f32[1,64,4]{2,1,0:T(8,128)S(1)}, f32[1,64,4]{2,1,0:T(8,128)S(1)}, u32[]{:S(2)}, u32[]{:S(2)}) collective-permute-start(f32[1,64,4]{2,1,0:T(8,128)S(1)} %get-tuple-element.16), channel_id=1, source_target_pairs={{1,0},{2,1},{3,2},{4,3},{5,4},{6,5},{7,6},{9,8},{10,9},{11,10},{12... | collective-permute-start | bytes 3080 | tf_op jit(solution)/shard_map/ppermute | solution.py:36
  15.2 9.5 %copy-start.7 = (f32[1,64,512]{2,1,0:T(8,128)S(1)}, f32[1,64,512]{2,1,0:T(8,128)}, u32[]{:S(2)}) copy-start(f32[1,64,512]{2,1,0:T(8,128)} %param.7) | copy-start | bytes 393220
  15.2 9.5 %copy-start.12 = (f32[4,32,64]{2,1,0:T(8,128)S(1)}, f32[4,32,64]{2,1,0:T(8,128)}, u32[]{:S(2)}) copy-start(f32[4,32,64]{2,1,0:T(8,128)} %param.9) | copy-start | bytes 98308
  24.7 1.1 copy-start.18
  24.7 1.1 copy-start.20
  25.3 0.7 copy-start.4
  26.6 2.4 %copy-start.6 = (f32[1,32,1040]{2,1,0:T(8,128)}, f32[1,32,1040]{2,1,0:T(8,128)S(1)}, u32[]{:S(2)}) copy-start(f32[1,32,1040]{2,1,0:T(8,128)S(1)} %copy.17) | copy-start | bytes 399364
  31.3 5.9 %copy-start.9 = (f32[1,32,1040]{2,1,0:T(8,128)}, f32[1,32,1040]{2,1,0:T(8,128)S(1)}, u32[]{:S(2)}) copy-start(f32[1,32,1040]{2,1,0:T(8,128)S(1)} %get-tuple-element.74) | copy-start | bytes 399364
  38.2 2.0 %copy-start.15 = (f32[1,1040]{1,0:T(1,128)}, f32[1,1040]{1,0:T(1,128)S(1)}, u32[]{:S(2)}) copy-start(f32[1,1040]{1,0:T(1,128)S(1)} %squeeze.11) | copy-start | bytes 12484
  41.8 8.2 %collective-permute-start.2 = (f32[1,768]{1,0:T(1,128)}, f32[1,768]{1,0:T(1,128)S(1)}, u32[]{:S(2)}, u32[]{:S(2)}) collective-permute-start(f32[1,768]{1,0:T(1,128)} %slice.333), channel_id=1, source_target_pairs={{1,0},{2,1},{3,2},{4,3},{5,4},{6,5},{7,6},{9,8},{10,9},{11,10},{12... | collective-permute-start | bytes 9224 | tf_op jit(solution)/shard_map/ppermute | solution.py:46
  45.9 3.8 %copy-start.2 = (f32[256,128]{1,0:T(8,128)S(1)}, f32[256,128]{1,0:T(8,128)}, u32[]{:S(2)}) copy-start(f32[256,128]{1,0:T(8,128)} %get-tuple-element.75) | copy-start | bytes 393220
  45.9 3.8 %copy-start.3 = (f32[256,128]{1,0:T(8,128)S(1)}, f32[256,128]{1,0:T(8,128)}, u32[]{:S(2)}) copy-start(f32[256,128]{1,0:T(8,128)} %get-tuple-element.76) | copy-start | bytes 393220
  45.9 4.1 %copy-start.17 = (f32[1,1024]{1,0:T(1,128)S(1)}, f32[1,1024]{1,0:T(1,128)}, u32[]{:S(2)}) copy-start(f32[1,1024]{1,0:T(1,128)} %get-tuple-element.53) | copy-start | bytes 12292
  45.9 4.5 %copy-start.33 = (f32[64]{0:T(128)S(1)}, f32[64]{0:T(128)}, u32[]{:S(2)}) copy-start(f32[64]{0:T(128)} %get-tuple-element.69) | copy-start | bytes 772
  45.9 4.5 %copy-start.34 = (f32[64]{0:T(128)S(1)}, f32[64]{0:T(128)}, u32[]{:S(2)}) copy-start(f32[64]{0:T(128)} %get-tuple-element.70) | copy-start | bytes 772
  51.6 20.1 %collective-permute-start.5 = (f32[1,768]{1,0:T(1,128)S(1)}, f32[1,768]{1,0:T(1,128)S(1)}, u32[]{:S(2)}, u32[]{:S(2)}) collective-permute-start(f32[1,768]{1,0:T(1,128)S(1)} %pad.112), channel_id=1, source_target_pairs={{0,1},{1,2},{2,3},{3,4},{4,5},{5,6},{6,7},{8,9},{9,10},{10,11},{11... | collective-permute-start | bytes 9224 | tf_op jit(solution)/shard_map/ppermute | solution.py:46
  57.8 3.7 %copy-start.31 = (f32[64]{0:T(128)S(1)}, f32[64]{0:T(128)}, u32[]{:S(2)}) copy-start(f32[64]{0:T(128)} %get-tuple-element.67) | copy-start | bytes 772
  57.9 3.7 %copy-start.32 = (f32[64]{0:T(128)S(1)}, f32[64]{0:T(128)}, u32[]{:S(2)}) copy-start(f32[64]{0:T(128)} %get-tuple-element.68) | copy-start | bytes 772
  61.5 1.6 copy-start.1
  63.1 30.0 %copy-start.30 = (f32[1,3]{1,0:T(1,128)S(1)}, f32[1,3]{1,0:T(1,128)}, u32[]{:S(2)}) copy-start(f32[1,3]{1,0:T(1,128)} %constant.211) | copy-start | bytes 40
  63.1 31.3 %copy-start.16 = (f32[1,1040]{1,0:T(1,128)S(1)}, f32[1,1040]{1,0:T(1,128)}, u32[]{:S(2)}) copy-start(f32[1,1040]{1,0:T(1,128)} %copy-done.15) | copy-start | bytes 12484
  63.1 31.3 %copy-start.22 = (f32[1,1024]{1,0:T(1,128)S(1)}, f32[1,1024]{1,0:T(1,128)}, u32[]{:S(2)}) copy-start(f32[1,1024]{1,0:T(1,128)} %param.8) | copy-start | bytes 12292
  63.1 40.3 %copy-start.23 = (f32[32]{0:T(128)S(1)}, f32[32]{0:T(128)}, u32[]{:S(2)}) copy-start(f32[32]{0:T(128)} %get-tuple-element.54) | copy-start | bytes 388
  63.1 40.4 %copy-start.24 = (f32[32]{0:T(128)S(1)}, f32[32]{0:T(128)}, u32[]{:S(2)}) copy-start(f32[32]{0:T(128)} %get-tuple-element.55) | copy-start | bytes 388
  63.2 40.4 %copy-start.25 = (f32[32]{0:T(128)S(1)}, f32[32]{0:T(128)}, u32[]{:S(2)}) copy-start(f32[32]{0:T(128)} %get-tuple-element.56) | copy-start | bytes 388
  63.2 40.4 %copy-start.26 = (f32[32]{0:T(128)S(1)}, f32[32]{0:T(128)}, u32[]{:S(2)}) copy-start(f32[32]{0:T(128)} %get-tuple-element.57) | copy-start | bytes 388
  63.2 40.4 %copy-start.27 = (f32[32]{0:T(128)S(1)}, f32[32]{0:T(128)}, u32[]{:S(2)}) copy-start(f32[32]{0:T(128)} %get-tuple-element.58) | copy-start | bytes 388
  63.2 40.4 %copy-start.28 = (f32[32]{0:T(128)S(1)}, f32[32]{0:T(128)}, u32[]{:S(2)}) copy-start(f32[32]{0:T(128)} %get-tuple-element.59) | copy-start | bytes 388
  63.2 40.4 %copy-start.29 = (f32[32]{0:T(128)S(1)}, f32[32]{0:T(128)}, u32[]{:S(2)}) copy-start(f32[32]{0:T(128)} %get-tuple-element.60) | copy-start | bytes 388
  63.2 40.5 %copy-start.10 = (f32[1,32,1040]{2,1,0:T(8,128)S(1)}, f32[1,32,1040]{2,1,0:T(8,128)}, u32[]{:S(2)}) copy-start(f32[1,32,1040]{2,1,0:T(8,128)} %copy-done.9) | copy-start | bytes 399364
  66.8 6.1 %collective-permute-start.4 = (f32[1,768]{1,0:T(1,128)S(1)}, f32[1,768]{1,0:T(1,128)S(1)}, u32[]{:S(2)}, u32[]{:S(2)}) collective-permute-start(f32[1,768]{1,0:T(1,128)S(1)} %slice.347), channel_id=1, source_target_pairs={{0,1},{1,2},{2,3},{3,4},{4,5},{5,6},{6,7},{8,9},{9,10},{10,11},{11... | collective-permute-start | bytes 9224 | tf_op jit(solution)/shard_map/ppermute | solution.py:46
  75.6 3.8 %collective-permute-start.6 = (f32[1,3]{1,0:T(1,128)S(1)}, f32[1,3]{1,0:T(1,128)S(1)}, u32[]{:S(2)}, u32[]{:S(2)}) collective-permute-start(f32[1,3]{1,0:T(1,128)S(1)} %pad_maximum_fusion.16), channel_id=1, source_target_pairs={{0,1},{1,0},{2,3},{3,2},{4,5},{5,4},{6,7},{7,6},{8,9},{9,8},{10,11... | collective-permute-start | bytes 44 | tf_op jit(solution)/shard_map/ppermute | solution.py:18
  81.5 5.0 %collective-permute-start.7 = (f32[1,3]{1,0:T(1,128)S(1)}, f32[1,3]{1,0:T(1,128)S(1)}, u32[]{:S(2)}, u32[]{:S(2)}) collective-permute-start(f32[1,3]{1,0:T(1,128)S(1)} %fusion.300), channel_id=1, source_target_pairs={{0,2},{1,3},{2,0},{3,1},{4,6},{5,7},{6,4},{7,5},{8,10},{9,11},{10,... | collective-permute-start | bytes 44 | tf_op jit(solution)/shard_map/ppermute | solution.py:18
  88.6 4.6 %collective-permute-start.8 = (f32[1,3]{1,0:T(1,128)S(1)}, f32[1,3]{1,0:T(1,128)S(1)}, u32[]{:S(2)}, u32[]{:S(2)}) collective-permute-start(f32[1,3]{1,0:T(1,128)S(1)} %fusion.301), channel_id=1, source_target_pairs={{0,4},{1,5},{2,6},{3,7},{4,0},{5,1},{6,2},{7,3},{8,12},{9,13},{10,... | collective-permute-start | bytes 44 | tf_op jit(solution)/shard_map/ppermute | solution.py:18
  95.9 5.8 %collective-permute-start.10 = (f32[1,1,8]{2,1,0:T(1,128)S(1)}, f32[1,1,8]{2,1,0:T(1,128)S(1)}, u32[]{:S(2)}, u32[]{:S(2)}) collective-permute-start(f32[1,1,8]{2,1,0:T(1,128)S(1)} %get-tuple-element.61), channel_id=1, source_target_pairs={{1,0},{2,1},{3,2},{4,3},{5,4},{6,5},{7,6},{9,8},{10,9},{11,10},{12... | collective-permute-start | bytes 104 | tf_op jit(solution)/shard_map/ppermute | solution.py:36
  97.2 5.8 %collective-permute-start.9 = (f32[1,1,8]{2,1,0:T(1,128)S(1)}, f32[1,1,8]{2,1,0:T(1,128)S(1)}, u32[]{:S(2)}, u32[]{:S(2)}) collective-permute-start(f32[1,1,8]{2,1,0:T(1,128)S(1)} %get-tuple-element.62), channel_id=1, source_target_pairs={{0,1},{1,2},{2,3},{3,4},{4,5},{5,6},{6,7},{8,9},{9,10},{10,11},{11... | collective-permute-start | bytes 104 | tf_op jit(solution)/shard_map/ppermute | solution.py:34
  103.1 2.5 %copy-start.14 = (f32[3,16,32]{2,1,0:T(8,128)S(1)}, f32[3,16,32]{2,1,0:T(8,128)}, u32[]{:S(2)}) copy-start(f32[3,16,32]{2,1,0:T(8,128)} %param.10) | copy-start | bytes 18436
  103.7 3.0 %copy-start.11 = (f32[1,1,32,1040]{3,2,1,0:T(8,128)S(1)}, f32[1,1,32,1040]{3,2,1,0:T(8,128)}, u32[]{:S(2)}) copy-start(f32[1,1,32,1040]{3,2,1,0:T(8,128)} %copy.20) | copy-start | bytes 399364
  104.5 2.7 %copy-start.5 = (f32[1,64,519]{2,1,0:T(8,128)S(1)}, f32[1,64,519]{2,1,0:T(8,128)}, u32[]{:S(2)}) copy-start(f32[1,64,519]{2,1,0:T(8,128)} %copy-done.4) | copy-start | bytes 398596
  104.9 2.7 %copy-start.8 = (f32[1,64,512]{2,1,0:T(8,128)S(1)}, f32[1,64,512]{2,1,0:T(8,128)}, u32[]{:S(2)}) copy-start(f32[1,64,512]{2,1,0:T(8,128)} %param.7) | copy-start | bytes 393220
  105.0 2.7 %copy-start.19 = (f32[1,64,4]{2,1,0:T(8,128)S(1)}, f32[1,64,4]{2,1,0:T(8,128)}, u32[]{:S(2)}) copy-start(f32[1,64,4]{2,1,0:T(8,128)} %copy-done.18) | copy-start | bytes 3076
  105.0 2.7 %copy-start.21 = (f32[1,64,4]{2,1,0:T(8,128)S(1)}, f32[1,64,4]{2,1,0:T(8,128)}, u32[]{:S(2)}) copy-start(f32[1,64,4]{2,1,0:T(8,128)} %copy-done.20) | copy-start | bytes 3076
  107.3 53.7 %copy-start.13 = (f32[4,32,64]{2,1,0:T(8,128)S(1)}, f32[4,32,64]{2,1,0:T(8,128)}, u32[]{:S(2)}) copy-start(f32[4,32,64]{2,1,0:T(8,128)} %param.9) | copy-start | bytes 98308
